TPU v7x, 32 devices: a whole 2x2x4 slice. The times are simulated.
32 devices in a mesh: row: 2 (over x), col: 4 (over z), freq: 4 (over y, core).
Axes of the slice: x: 2, y: 2, z: 4, core: 2. Of those that a mesh axis runs over, the one named last changes fastest.
Arguments:
- data: bfloat16 [2, 4, 2048, 2048], P(None, 'freq', 'row', 'col'), may hold values from -4.7729708 to 4.7729708, as said below
- primaries: bfloat16 [2, 4, 2048, 2048], P(None, 'freq', 'row', 'col'), may hold values from -6 to 6
Outputs:
- updated_primaries: bfloat16 [2, 4, 2048, 2048], P(None, 'freq', 'row', 'col')
- updated_residual: float32 [2, 4, 2048, 2048], P(None, 'freq', 'row', 'col')
Inputs may be any that keep to these rules, and one draw needn't show every extreme that they name: `data`: magnitudes vary by source, receiver and frequency.
All inputs are finite; a program needn't handle non-finite values.
Results may differ from a plain program's by a relative error of at most 0.0045.
Values may be sent and summed in bfloat16 or wider, within the bound.
No kernel may reach another device: no remote copies, remote signals or barrier semaphores. Data moves between devices by JAX's collectives and lax.ppermute only.
A program may use at most 128 MiB of HBM per device.

v0:
```python
import jax
import jax.numpy as jnp
from jax import lax
from jax.sharding import PartitionSpec as P


def batched(left, right):
    return jnp.einsum("fik,fkj->fij", left, right, preferred_element_type=jnp.float32)


def complex_product(left, right):
    real = batched(left[0], right[0]) - batched(left[1], right[1])
    imag = batched(left[0], right[1]) + batched(left[1], right[0])
    return jnp.stack([real, imag])


def gradient_step(data_part, primary_part):
    src_rows = data_part.shape[2]
    columns = lax.all_gather(data_part, "row", axis=2, tiled=True)

    def add_block(piece):
        return complex_product(piece, columns)

    forward = add_block(lax.all_gather(primary_part, "col", axis=3, tiled=True))
    residual = data_part.astype(jnp.float32) - primary_part.astype(jnp.float32) + forward
    rounded = residual.astype(jnp.bfloat16)
    real = jnp.einsum("fjk,fik->jfi", columns[0], rounded[0], preferred_element_type=jnp.float32)
    real = real + jnp.einsum(
        "fjk,fik->jfi", columns[1], rounded[1], preferred_element_type=jnp.float32
    )
    imag = jnp.einsum("fjk,fik->jfi", columns[0], rounded[1], preferred_element_type=jnp.float32)
    imag = imag - jnp.einsum(
        "fjk,fik->jfi", columns[1], rounded[0], preferred_element_type=jnp.float32
    )
    summed = lax.psum_scatter(
        jnp.concatenate([real, imag], axis=2), "col", scatter_dimension=0, tiled=True
    )
    adjoint = jnp.stack([summed[:, :, :src_rows], summed[:, :, src_rows:]]).transpose(0, 2, 3, 1)
    gradient = (adjoint - residual).astype(jnp.bfloat16)
    moved = add_block(lax.all_gather(gradient, "col", axis=3, tiled=True))
    change = moved - gradient.astype(jnp.float32)
    return (residual, gradient, change)


def local(data, primaries):
    res, grad, chg = gradient_step(data, primaries)
    inner_local = jnp.sum(chg * res)
    energy_local = jnp.sum(chg * chg)
    inner, energy = lax.psum((inner_local, energy_local), ("row", "col", "freq"))
    step = -inner / (energy + 1e-06)
    updated_primaries = (primaries.astype(jnp.float32) + step * grad.astype(jnp.float32)).astype(
        jnp.bfloat16
    )
    updated_residual = res + step * chg
    return (updated_primaries, updated_residual)


def solution(mesh):
    in_specs = (P(None, "freq", "row", "col"), P(None, "freq", "row", "col"))
    out_specs = (P(None, "freq", "row", "col"), P(None, "freq", "row", "col"))
    return jax.shard_map(local, mesh=mesh, in_specs=in_specs, out_specs=out_specs, check_vma=False)
```

profile of v0, /device:TPU:12, one launch (start us, length us, event | category | flops | bytes accessed | tf_op | source)
XLA Modules:
  0.0 759.2 jit_solution(8041567438124025095)
XLA Ops:
  8.7 58.7 %all-gather.6.cloned.1.call-done = bf16[2,1,2048,512]{3,2,1,0:T(8,128)(2,1)} async-done(((bf16[2,1,1024,512]{3,2,1,0:T(8,128)(2,1)}), bf16[2,1,2048,512]{3,2,1,0:T(8,128)(2,1)}) %all-gather.6.cloned.1.call-update) | async-done | bytes 4194320 | tf_op jit(solution)/shard_map/all_gather | solution.py:19
  67.4 148.5 %all-gather.4.cloned.1.call-done = bf16[2,1,1024,2048]{3,2,1,0:T(8,128)(2,1)} async-done(((bf16[2,1,1024,512]{3,2,1,0:T(8,128)(2,1)}), bf16[2,1,1024,2048]{3,2,1,0:T(8,128)(2,1)}) %all-gather.4.cloned.1.call-update) | async-done | bytes 8388624 | tf_op jit(solution)/shard_map/all_gather | solution.py:24
  215.9 5.3 fusion.4
  222.4 2.3 fusion.5
  224.7 2.3 add_bitcast_fusion.2
  227.1 2.3 subtract_bitcast_fusion.2
  229.4 3.1 fusion.14
  232.5 2.4 fusion.13
  234.8 2.4 fusion.12
  237.2 2.4 subtract_bitcast_fusion
  239.6 2.5 add_bitcast_fusion
  242.1 6.2 pad_maximum_fusion
  248.4 278.6 %reduce-scatter.2.cloned.1.call-done = f32[512,1,2048]{0,2,1:T(8,128)} async-done(((f32[2048,1,2048]{0,2,1:T(8,128)}), f32[512,1,2048]{0,2,1:T(8,128)}) %reduce-scatter.2.cloned.1.call-update) | async-done | bytes 4194320 | tf_op jit(solution)/shard_map/reduce_scatter | solution.py:35
  527.0 2.8 slice_bitcast_fusion.13
  529.8 1.4 copy-done.2
  531.2 2.2 fusion.3
  533.4 150.5 %all-gather.8.cloned.1.call-done = bf16[2,1,1024,2048]{3,2,1,0:T(8,128)(2,1)} async-done(((bf16[2,1,1024,512]{3,2,1,0:T(8,128)(2,1)}), bf16[2,1,1024,2048]{3,2,1,0:T(8,128)(2,1)}) %all-gather.8.cloned.1.call-update) | async-done | bytes 8388624 | tf_op jit(solution)/shard_map/all_gather | solution.py:40
  684.0 5.3 fusion.8
  690.4 2.3 fusion.9
  692.7 2.3 add_bitcast_fusion.1
  695.1 2.3 subtract_bitcast_fusion.1
  698.7 2.3 multiply_reduce_fusion
  700.9 43.2 %all-reduce = (f32[]{:T(128)}, f32[]{:T(128)}) all-reduce(f32[]{:T(128)} %get-tuple-element.3, f32[]{:T(128)} %get-tuple-element.2), channel_id=1, replica_groups=mesh['row'=2,'col'=4,'freq'=4] {'row','col','freq'}, use_global_device_ids=true, to_apply=%region_2.0 | all-reduce | flops 2 | bytes 16 | tf_op jit(solution)/shard_map/psum | solution.py:49
  745.5 7.2 multiply_add_fusion
  (31 shorter events, 5.0 us)
Async XLA Ops:
  7.2 60.3 %all-gather.6.cloned.1.call-start = ((), (), s32[]{:S(2)}) async-start(), calls=%async_computation.2 | async-start | bytes 6291456 | tf_op jit(solution)/shard_map/all_gather | solution.py:19
  7.9 208.0 %all-gather.4.cloned.1.call-start = ((), (), s32[]{:S(2)}) async-start(), calls=%async_computation.1 | async-start | bytes 10485760 | tf_op jit(solution)/shard_map/all_gather | solution.py:24
  8.6 518.3 %reduce-scatter.2.cloned.1.call-start = ((), (), s32[]{:S(2)}) async-start(), calls=%async_computation.3 | async-start | bytes 20971520 | tf_op jit(solution)/shard_map/reduce_scatter | solution.py:35
  215.9 5.4 copy-start.8
  215.9 6.4 copy-start.10
  227.0 2.4 copy-start.4
  227.0 2.4 copy-start.7
  248.4 435.6 %all-gather.8.cloned.1.call-start = ((), (), s32[]{:S(2)}) async-start(), calls=%async_computation.4 | async-start | bytes 10485760 | tf_op jit(solution)/shard_map/all_gather | solution.py:40
  527.0 4.2 copy-start
  529.8 1.4 copy-start.2
  684.0 5.3 copy-start.9
  684.0 6.4 copy-start.11
  695.1 2.4 copy-start.5
  695.1 2.9 copy-start.1
  695.1 3.6 copy-start.3
  698.7 2.3 copy-start.6
Sparse Core Ops, SparseCore 0:
  9.5 57.8 all-gather.5
  69.0 146.8 all-gather.3
  248.5 278.4 reduce-scatter.1
  533.5 150.3 all-gather.7
where the time goes:
time: 760 us; the launch traced here: 759 us
  waiting for transfers between devices  638 us (84%)
  blocking collectives  43.2 us (6%)
  matrix products  34.3 us (5%)
  other arithmetic  20.9 us (3%)
  between operations  15.2 us (2%)
  local copies, waits for them, and re-layouts  7.68 us (1%)
    reduce_scatter x1, waiting for transfers between devices, gradient_step(): lax.psum_scatter(jnp.concatenate([real, imag], axis=2), 'col', scatter_di...  279 us
    all_gather x1, waiting for transfers between devices, gradient_step(): moved = add_block(lax.all_gather(gradient, 'col', axis=3, tiled=True))  151 us
    all_gather x1, waiting for transfers between devices, gradient_step(): forward = add_block(lax.all_gather(primary_part, 'col', axis=3, tiled=True))  148 us
    all_gather x1, waiting for transfers between devices, gradient_step(): columns = lax.all_gather(data_part, 'row', axis=2, tiled=True)  58.7 us
    psum x1, blocking collectives, local(): lax.psum((inner_local, energy_local), ('row', 'col', 'freq'))  43.2 us
    dot_general x8, matrix products, batched(): jnp.einsum('fik,fkj->fij', left, right, preferred_element_type=jnp.float32)  24.6 us
  transfers between devices with their start and end apart: 4, of which 4 were waited for; matrix products, arithmetic and copies ran while one was open for 0% of the time, Pallas kernels for 0%

commit v1 on v0

--- a/solution.py
+++ b/solution.py
@@ -2,6 +2,27 @@
 import jax.numpy as jnp
 from jax import lax
 from jax.sharding import PartitionSpec as P
+
+
+def collect(value, axis, dim):
+    size, mine, extent = (lax.axis_size(axis), lax.axis_index(axis), value.shape[dim])
+    ahead = [(i, (i + 1) % size) for i in range(size)]
+    left = [(i, (i - 1) % size) for i in range(size)]
+    out = jnp.zeros((*value.shape[:dim], size * extent, *value.shape[dim + 1 :]), value.dtype)
+    out = lax.dynamic_update_slice_in_dim(out, value, mine * extent, axis=dim)
+    from_left = from_right = value
+    middle = size // 2
+    for step in range(1, middle + 1):
+        from_left = lax.ppermute(from_left, axis, ahead)
+        out = lax.dynamic_update_slice_in_dim(
+            out, from_left, (mine - step) % size * extent, axis=dim
+        )
+        if step < size - middle:
+            from_right = lax.ppermute(from_right, axis, left)
+            out = lax.dynamic_update_slice_in_dim(
+                out, from_right, (mine + step) % size * extent, axis=dim
+            )
+    return out
 
 
 def batched(left, right):
@@ -37,7 +58,7 @@
     )
     adjoint = jnp.stack([summed[:, :, :src_rows], summed[:, :, src_rows:]]).transpose(0, 2, 3, 1)
     gradient = (adjoint - residual).astype(jnp.bfloat16)
-    moved = add_block(lax.all_gather(gradient, "col", axis=3, tiled=True))
+    moved = add_block(collect(gradient, "col", 3))
     change = moved - gradient.astype(jnp.float32)
     return (residual, gradient, change)
 

time: 760 us -> 765 us (level)
  waiting for transfers between devices: 638 us -> 615 us
  local copies, waits for them, and re-layouts: 7.68 us -> 19.4 us
    all_gather x1 -> x0, waiting for transfers between devices: 151 us -> none  [gradient_step(): moved = add_block(lax.all_gather(gradient, 'col', axis=3, tiled=True))]
    ppermute x0 -> x3, waiting for transfers between devices: none -> 128 us  [the longest x2 128 us: collect(): from_left = lax.ppermute(from_left, axis, ahead)]
    dynamic_update_slice x0 -> x3, local copies, waits for them, and re-layouts: none -> 9.6 us  [the longest x2 6.27 us: collect(): lax.dynamic_update_slice_in_dim(out, from_left, (mine - step) % size * ex...]
  transfers between devices with their start and end apart: 4 -> 6, of which waited for: 4 -> 5; matrix products, arithmetic and copies ran while one was open for 0% -> 1% of each run, Pallas kernels for 0% -> 0%
where the time goes in v1:
time: 765 us; the launch traced here: 763 us
  waiting for transfers between devices  615 us (80%)
  blocking collectives  41.4 us (5%)
  matrix products  40.2 us (5%)
  other arithmetic  23.9 us (3%)
  local copies, waits for them, and re-layouts  19.4 us (3%)
  between operations  15.2 us (2%)
    reduce_scatter x1, waiting for transfers between devices, gradient_step(): lax.psum_scatter(jnp.concatenate([real, imag], axis=2), 'col', scatter_di...  279 us
    all_gather x1, waiting for transfers between devices, gradient_step(): forward = add_block(lax.all_gather(primary_part, 'col', axis=3, tiled=True))  148 us
    ppermute x2, waiting for transfers between devices, collect(): from_left = lax.ppermute(from_left, axis, ahead)  128 us
    all_gather x1, waiting for transfers between devices, gradient_step(): columns = lax.all_gather(data_part, 'row', axis=2, tiled=True)  58.7 us
    psum x1, blocking collectives, local(): lax.psum((inner_local, energy_local), ('row', 'col', 'freq'))  41.4 us
    dot_general x8, matrix products, batched(): jnp.einsum('fik,fkj->fij', left, right, preferred_element_type=jnp.float32)  23.9 us
  transfers between devices with their start and end apart: 6, of which 5 were waited for; matrix products, arithmetic and copies ran while one was open for 1% of the time, Pallas kernels for 0%

profile of v1, /device:TPU:12, one launch (start us, length us, event | category | flops | bytes accessed | tf_op | source)
XLA Modules:
  0.0 763.0 jit_solution(1457570835469894639)
XLA Ops:
  8.7 58.7 %all-gather.5.cloned.1.call-done = bf16[2,1,2048,512]{3,2,1,0:T(8,128)(2,1)} async-done(((bf16[2,1,1024,512]{3,2,1,0:T(8,128)(2,1)}), bf16[2,1,2048,512]{3,2,1,0:T(8,128)(2,1)}) %all-gather.5.cloned.1.call-update) | async-done | bytes 4194320 | tf_op jit(solution)/shard_map/all_gather | solution.py:40
  67.4 148.5 %all-gather.3.cloned.1.call-done = bf16[2,1,1024,2048]{3,2,1,0:T(8,128)(2,1)} async-done(((bf16[2,1,1024,512]{3,2,1,0:T(8,128)(2,1)}), bf16[2,1,1024,2048]{3,2,1,0:T(8,128)(2,1)}) %all-gather.3.cloned.1.call-update) | async-done | bytes 8388624 | tf_op jit(solution)/shard_map/all_gather | solution.py:45
  215.9 5.3 fusion.5
  222.4 2.3 fusion.4
  229.4 3.1 fusion.15
  232.5 2.4 fusion.12
  234.8 5.6 fusion.13
  240.4 2.4 add_bitcast_fusion
  242.8 5.9 subtract_bitcast_fusion
  248.7 6.2 pad_maximum_fusion
  255.0 278.6 %reduce-scatter.2.cloned.1.call-done = f32[512,1,2048]{0,2,1:T(8,128)} async-done(((f32[2048,1,2048]{0,2,1:T(8,128)}), f32[512,1,2048]{0,2,1:T(8,128)}) %reduce-scatter.2.cloned.1.call-update) | async-done | bytes 4194320 | tf_op jit(solution)/shard_map/reduce_scatter | solution.py:56
  533.6 2.7 slice_bitcast_fusion.13
  540.8 3.2 copy-done.4
  544.0 5.0 collective-permute-start
  549.0 90.2 %collective-permute-done = bf16[2,1,1024,512]{3,2,1,0:T(8,128)(2,1)} collective-permute-done((bf16[2,1,1024,512]{3,2,1,0:T(8,128)(2,1)}, bf16[2,1,1024,512]{3,2,1,0:T(8,128)(2,1)}, u32[]{:S(2)}, u32[]{:S(2)}) %collective-permute-start) | collective-permute-done | bytes 2097184 | tf_op jit(solution)/shard_map/ppermute | solution.py:16
  639.2 2.5 collective-permute-start.2
  641.7 3.2 constant_dynamic-update-slice_fusion.2
  644.9 3.3 constant_dynamic-update-slice_fusion.1
  648.2 37.9 %collective-permute-done.2 = bf16[2,1,1024,512]{3,2,1,0:T(8,128)(2,1)} collective-permute-done((bf16[2,1,1024,512]{3,2,1,0:T(8,128)(2,1)}, bf16[2,1,1024,512]{3,2,1,0:T(8,128)(2,1)}, u32[]{:S(2)}, u32[]{:S(2)}) %collective-permute-start.2) | collective-permute-done | bytes 2097184 | tf_op jit(solution)/shard_map/ppermute | solution.py:16
  686.1 3.1 constant_dynamic-update-slice_fusion
  689.1 4.7 fusion.11
  701.4 4.2 multiply_reduce_fusion
  705.6 41.4 %all-reduce = (f32[]{:T(128)}, f32[]{:T(128)}) all-reduce(f32[]{:T(128)} %get-tuple-element.3, f32[]{:T(128)} %get-tuple-element.2), channel_id=1, replica_groups=mesh['row'=2,'col'=4,'freq'=4] {'row','col','freq'}, use_global_device_ids=true, to_apply=%region_2.3 | all-reduce | flops 2 | bytes 16 | tf_op jit(solution)/shard_map/psum | solution.py:70
  748.3 8.1 %multiply_add_fusion = (f32[2,1,1024,512]{3,2,1,0:T(8,128)}, bf16[2,1,1024,512]{3,2,1,0:T(8,128)(2,1)}) fusion(f32[2,1,1024,512]{3,2,1,0:T(8,128)} %get-tuple-element.9, f32[]{:T(128)S(6)} %div.3, bf16[2,1,1024,512]{3,2,1,0:T(8,128)(2,1)} %get-tuple-element.7, f32[1,1,1024,512]{3,2,1,0:T(8,128)} %copy-done.7, f32[1,1,1024,512]{3,2,1,0:T(8,128)} %copy-done.6, ...), kind=kLoop, calls=%fused_computation.16 | loop fusion | flops 9437184 | bytes 18874372 | tf_op jit(solution)/shard_map/add | solution.py:75
  (36 shorter events, 19.3 us)
Async XLA Ops:
  7.2 60.3 %all-gather.5.cloned.1.call-start = ((), (), s32[]{:S(2)}) async-start(), calls=%async_computation.2 | async-start | bytes 6291456 | tf_op jit(solution)/shard_map/all_gather | solution.py:40
  7.9 208.0 %all-gather.3.cloned.1.call-start = ((), (), s32[]{:S(2)}) async-start(), calls=%async_computation.1 | async-start | bytes 10485760 | tf_op jit(solution)/shard_map/all_gather | solution.py:45
  8.6 525.0 %reduce-scatter.2.cloned.1.call-start = ((), (), s32[]{:S(2)}) async-start(), calls=%async_computation.3 | async-start | bytes 20971520 | tf_op jit(solution)/shard_map/reduce_scatter | solution.py:56
  215.9 5.4 copy-start.8
  215.9 6.4 copy-start.9
  227.0 2.4 copy-start.2
  227.0 2.4 copy-start.3
  536.3 2.2 copy-start
  540.8 3.2 copy-start.4
  544.0 95.2 %collective-permute-start = (bf16[2,1,1024,512]{3,2,1,0:T(8,128)(2,1)}, bf16[2,1,1024,512]{3,2,1,0:T(8,128)(2,1)}, u32[]{:S(2)}, u32[]{:S(2)}) collective-permute-start(bf16[2,1,1024,512]{3,2,1,0:T(8,128)(2,1)} %get-tuple-element.7), channel_id=1, source_target_pairs={{0,4},{4,8},{8,12},{12,0},{1,5},{5,9},{9,13},{13,1},{2,6},{6,10},{... | collective-permute-start | bytes 6291464 | tf_op jit(solution)/shard_map/ppermute | solution.py:16
  549.0 95.9 %collective-permute-start.1 = (bf16[2,1,1024,512]{3,2,1,0:T(8,128)(2,1)}, bf16[2,1,1024,512]{3,2,1,0:T(8,128)(2,1)}, u32[]{:S(2)}, u32[]{:S(2)}) collective-permute-start(bf16[2,1,1024,512]{3,2,1,0:T(8,128)(2,1)} %get-tuple-element.7), channel_id=1, source_target_pairs={{0,12},{4,0},{8,4},{12,8},{1,13},{5,1},{9,5},{13,9},{2,14},{6,2},{... | collective-permute-start | bytes 6291464 | tf_op jit(solution)/shard_map/ppermute | solution.py:21
  639.2 46.9 %collective-permute-start.2 = (bf16[2,1,1024,512]{3,2,1,0:T(8,128)(2,1)}, bf16[2,1,1024,512]{3,2,1,0:T(8,128)(2,1)}, u32[]{:S(2)}, u32[]{:S(2)}) collective-permute-start(bf16[2,1,1024,512]{3,2,1,0:T(8,128)(2,1)} %collective-permute-done), channel_id=1, source_target_pairs={{0,4},{4,8},{8,12},{12,0},{1,5},{5,9},{9,13},{13,1},{2,6},{6,10},{... | collective-permute-start | bytes 6291464 | tf_op jit(solution)/shard_map/ppermute | solution.py:16
  644.9 44.3 %copy-start.10 = (bf16[2,1,2048,512]{3,2,1,0:T(8,128)(2,1)S(1)}, bf16[2,1,2048,512]{3,2,1,0:T(8,128)(2,1)}, u32[]{:S(2)}) copy-start(bf16[2,1,2048,512]{3,2,1,0:T(8,128)(2,1)} %all-gather.5.cloned.1.call-done) | copy-start | bytes 12582916
  689.1 4.7 copy-start.5
  698.5 2.4 copy-start.6
  698.5 2.9 copy-start.1
  701.4 4.2 copy-start.7
Sparse Core Ops, SparseCore 0:
  9.5 57.8 all-gather.4
  69.0 146.8 all-gather.2
  255.1 278.4 reduce-scatter.1
